TPU v7x, 256 devices: a whole 4x4x8 slice. The times are simulated.
256 devices in a mesh: row: 16 (over x, y_hi, core), col: 16 (over z, y_lo).
Axes of the slice: x: 4, y: 4 (y_hi: 2, y_lo: 2; y = y_hi * 2 + y_lo), z: 8, core: 2. Of those that a mesh axis runs over, the one named last changes fastest.
Arguments:
- panel_cols: bfloat16 [48, 4096, 512], P('col', 'row'), may hold values from -6 to 6
- inverses: bfloat16 [2, 256, 256], replicated, as said below
- trailing: bfloat16 [48, 4096, 4096], P(None, 'row', 'col'), may hold values from -6 to 6
Outputs:
- updated: bfloat16 [48, 4096, 4096], P(None, 'row', 'col')
Inputs may be any that keep to these rules, and one draw needn't show every extreme that they name: `inverses`: each of the two 256 x 256 matrices is lower triangular with a positive diagonal.
All inputs are finite; a program needn't handle non-finite values.
Results may differ from a plain program's by a relative error of at most 0.0063.
Values may be sent and summed in bfloat16 or wider, within the bound.
A program may use at most 128 MiB of HBM per device.

v0:
```python
import functools

import jax
import jax.numpy as jnp
from jax import lax
from jax.experimental import pallas as pl
from jax.experimental.pallas import tpu as pltpu
from jax.sharding import PartitionSpec as P

MESH = pl.DeviceIdType.MESH
TILE = 256
SHARED = 112
FIRST = 128
FEWER = 112
BEFORE = (3, 0)
PIECE = 16


def times_transposed(left, right):
    return lax.dot_general(left, right, (((1,), (1,)), ((), ())), preferred_element_type=jnp.float32)


def kernel(
    panel, inverses, trailing, window,
    own, mate, shared, sums_in, sums_out, stage, couple_piece, pieces, couple, keys,
    ring_send, ring_recv, mate_send, mate_recv, sum_send, sum_recv,
    load_sem, piece_sem, spread_sem, ready_sem,
):
    row, col = lax.axis_index("row"), lax.axis_index("col")
    z, y = col // 2, lax.rem(col, 2)
    chip, core = row // 2, lax.rem(row, 2)
    my_piece = core * PIECE + chip * 2 + y
    mate_dev = (row, col + 1 - 2 * y)
    core_dev = (row + 1 - 2 * core, col)
    ring_dev = ((row, lax.rem(col + 2, 16)), (row, lax.rem(col + 14, 16)))
    plain = TILE - SHARED

    load_own = pltpu.make_async_copy(panel, own.at[z], load_sem.at[0])
    load_window = pltpu.make_async_copy(trailing, window, load_sem.at[1])
    load_own.start()
    load_window.start()

    def plane_device(q, plane):
        at = lax.rem(q, PIECE)
        return ((at // 2) * 2 + q // PIECE, plane * 2 + lax.rem(at, 2))

    key_plane = lax.rem(row + 14, 16) // 2
    is_source = col == 0
    is_couple = jnp.logical_and(is_source, row == 1)

    barrier = pltpu.get_barrier_semaphore()

    def greet(dev):
        pl.semaphore_signal(barrier, inc=1, device_id=dev, device_id_type=MESH)

    @pl.when(z == 0)
    def _():
        def greet_place(place, carry):
            greet((row, place * 2 + y))
            return carry

        lax.fori_loop(1, 8, greet_place, 0)

    @pl.when(jnp.logical_and(z > 0, z < 6))
    def _():
        greet(ring_dev[0])

    @pl.when(z > 2)
    def _():
        greet(ring_dev[1])

    def greet_plane(p, carry):
        @pl.when(core * PIECE + p != my_piece)
        def _():
            greet(plane_device(core * PIECE + p, z))

        return carry

    lax.fori_loop(0, PIECE, greet_plane, 0)
    greet(core_dev)

    @pl.when(jnp.logical_and(jnp.logical_and(z == 0, core == 0), row + col > 0))
    def _():
        greet((1, 0))

    beside = jnp.logical_or(z == 1, z == 7)
    from_others = jnp.where(z == 0, 0, jnp.where(beside, 1, 3))
    pl.semaphore_wait(barrier, 16 + from_others + jnp.where(is_couple, 15, 0))

    @pl.when(z != 0)
    def _():
        pl.semaphore_signal(
            ready_sem.at[jnp.where(z == 1, 0, jnp.where(z == 7, 2, 1))], inc=1, device_id=(row, y), device_id_type=MESH
        )

    @pl.when(z == 2)
    def _():
        pl.semaphore_signal(ready_sem.at[3], inc=1, device_id=ring_dev[1], device_id_type=MESH)

    @pl.when(z == 6)
    def _():
        pl.semaphore_signal(ready_sem.at[3], inc=1, device_id=ring_dev[0], device_id_type=MESH)

    load_own.wait()

    def is_shared(unit):
        return isinstance(unit, int) and unit == 3

    def ring_ref(d, s, unit):
        place = lax.rem(z + 8 - s, 8) if d == 0 else lax.rem(z + s, 8)
        return shared.at[place] if is_shared(unit) else own.at[place, unit]

    def ring_copy(d, s, unit, up=None):
        ref = ring_ref(d, s, unit)
        if up is not None:
            rows = SHARED if is_shared(unit) else TILE
            up = up * rows // TILE // 16 * 16
            ref = ref.at[pl.ds(0, up)] if d == 0 else ref.at[pl.ds(up, rows - up)]
        return pltpu.make_async_remote_copy(
            ref, ref, ring_send.at[d, s, unit], ring_recv.at[d, s, unit],
            device_id=ring_dev[d], device_id_type=MESH,
        )

    def arrived(d, s, unit, up=None):
        ref = ring_ref(d, s, unit)
        if up is not None:
            rows = SHARED if is_shared(unit) else TILE
            up = up * rows // TILE // 16 * 16
            ref = ref.at[pl.ds(0, up)] if d == 0 else ref.at[pl.ds(up, rows - up)]
        pltpu.make_async_remote_copy(
            ref, ref, ring_send.at[d, s - 1, unit], ring_recv.at[d, s - 1, unit],
            device_id=ring_dev[d], device_id_type=MESH,
        ).wait_recv()

    def opposite(place, action):
        @pl.when(place == 1)
        def _():
            action(FEWER)

        @pl.when(place == 7)
        def _():
            action(TILE - FEWER)

        @pl.when(jnp.logical_and(place != 1, place != 7))
        def _():
            action(TILE // 2)

    next_place = (lax.rem(z + 1, 8), lax.rem(z + 7, 8))

    def mate_copy(unit):
        if unit == 3:
            ref, dst = own.at[z, 2, pl.ds(plain, SHARED)], shared.at[z]
        else:
            ref, dst = own.at[z, unit], mate.at[unit]
        return pltpu.make_async_remote_copy(
            ref, dst, mate_send.at[unit], mate_recv.at[unit], device_id=mate_dev, device_id_type=MESH
        )

    key_tile = jnp.where(row < 2, 1, 0)

    @pl.when(is_couple)
    def _():
        def send(q, carry):
            src = own.at[0, 0, pl.ds(lax.rem(q, PIECE) * 16, 16), pl.ds((q // PIECE) * 128, 128)]

            @pl.when(q != my_piece)
            def _():
                pltpu.make_async_remote_copy(
                    src, couple_piece, piece_sem.at[2], piece_sem.at[3], device_id=plane_device(q, 0),
                    device_id_type=MESH,
                ).start()

            @pl.when(q == my_piece)
            def _():
                pltpu.make_async_copy(src, couple_piece, piece_sem.at[3]).start()

            return carry

        lax.fori_loop(0, 2 * PIECE, send, 0)

    @pl.when(is_source)
    def _():
        def send(p, carry):
            q = core * PIECE + p
            src = own.at[0, key_tile, pl.ds(p * 16, 16)]
            dst = stage.at[key_plane, :, pl.ds(0, 512)]

            @pl.when(q != my_piece)
            def _():
                pltpu.make_async_remote_copy(
                    src, dst, piece_sem.at[0], piece_sem.at[1], device_id=plane_device(q, 0), device_id_type=MESH
                ).start()

            @pl.when(q == my_piece)
            def _():
                pltpu.make_async_copy(src, dst, piece_sem.at[1]).start()

            return carry

        lax.fori_loop(0, PIECE, send, 0)

    def begin(units, ways=(0, 1)):
        for unit in units:
            for d in ways:
                ring_copy(d, 0, unit).start()

    def begin_part(start, rows, ways=(0, 1)):
        if rows:
            for d in ways:
                ref = own.at[z, 0, pl.ds(start, rows)]
                pltpu.make_async_remote_copy(
                    ref, ref, ring_send.at[d, 0, 0], ring_recv.at[d, 0, 0], device_id=ring_dev[d], device_id_type=MESH
                ).start()

    mine = pieces.at[my_piece]

    def spread():
        def send(p, carry):
            q = core * PIECE + p

            @pl.when(q != my_piece)
            def _():
                pltpu.make_async_remote_copy(
                    mine, mine, spread_sem.at[0], spread_sem.at[1], device_id=plane_device(q, z), device_id_type=MESH
                ).start()

            return carry

        lax.fori_loop(0, PIECE, send, 0)
        for unit in (0, 1):
            if unit not in BEFORE:
                mate_copy(unit).start()

    def begin_mate():
        for unit in BEFORE:
            mate_copy(unit).start()

    @pl.when(z == 0)
    def _():
        begin_mate()
        pl.semaphore_wait(ready_sem.at[0], 1)
        begin_part(0, FIRST, (0,))
        pl.semaphore_wait(ready_sem.at[2], 1)
        begin_part(0, FIRST, (1,))
        staged = stage.at[:, :, pl.ds(0, 512)]
        pltpu.make_async_copy(couple_piece, couple_piece, piece_sem.at[3]).wait()
        pltpu.make_async_copy(staged, staged, piece_sem.at[1]).wait()
        for plane in range(8):
            stage[plane, :, 512:640] = couple_piece[...]
        pieces[my_piece] = stage[0]
        pl.semaphore_wait(ready_sem.at[1], 5)

        def send(plane, carry):
            pltpu.make_async_remote_copy(
                stage.at[plane], mine, piece_sem.at[4], piece_sem.at[5], device_id=(row, plane * 2 + y),
                device_id_type=MESH,
            ).start()
            return carry

        lax.fori_loop(1, 8, send, 0)
        begin_part(FIRST, TILE - FIRST)
        begin((1, 2))
        spread()

    def begin_beside(inward, outward):
        begin((0,), (inward,))
        begin_mate()
        begin((1, 2), (inward,))
        pl.semaphore_wait(ready_sem.at[3], 1)
        begin((0, 1, 2), (outward,))

    @pl.when(z == 1)
    def _():
        begin_beside(1, 0)

    @pl.when(z == 7)
    def _():
        begin_beside(0, 1)

    @pl.when(jnp.logical_and(z > 1, z < 7))
    def _():
        begin((0,))
        begin_mate()
        begin((1, 2))

    mate_copy(3).wait_recv()
    begin((3,))

    @pl.when(z != 0)
    def _():
        pltpu.make_async_copy(mine, mine, piece_sem.at[5]).wait()
        spread()

    peers = pieces.at[pl.ds(0, PIECE - 1)]
    half = pieces.at[pl.ds(core * PIECE, PIECE)]
    swap = pltpu.make_async_remote_copy(
        half, half, spread_sem.at[2], spread_sem.at[3], device_id=core_dev, device_id_type=MESH
    )

    for d in (0, 1):
        arrived(d, 1, 0)
        ring_copy(d, 1, 0).start()
    pltpu.make_async_copy(peers, peers, spread_sem.at[1]).wait()
    swap.start()
    for unit in (1, 2):
        for d in (0, 1):
            arrived(d, 1, unit)
            ring_copy(d, 1, unit).start()
    swap.wait_recv()

    for part in (0, 1):
        raw = pieces[part * PIECE:(part + 1) * PIECE, :, 512:640].reshape(TILE, 128)
        keys[0, :, part * 128:(part + 1) * 128] = raw
    couple[...] = times_transposed(keys[0, :, 0:TILE], inverses[0]).astype(jnp.bfloat16)

    def factor(raw):
        left = times_transposed(raw[:, 0:TILE], inverses[0]).astype(jnp.bfloat16)
        reduced = (raw[:, TILE:].astype(jnp.float32) - times_transposed(left, couple[...])).astype(jnp.bfloat16)
        right = times_transposed(reduced, inverses[1]).astype(jnp.bfloat16)
        return left, right

    def product(factors, which):
        left, right = factors
        return times_transposed(left, keys[which, :, 0:TILE]) + times_transposed(right, keys[which, :, TILE:])

    for which in (0, 1):
        parity = y if which == 0 else 1 - y
        raw = pieces[pl.ds(parity * PIECE, PIECE), :, 0:512].reshape(TILE, 2 * TILE)
        left, right = factor(raw)
        keys[which, :, 0:TILE] = left
        keys[which, :, TILE:] = right

    load_window.wait()

    def subtract(tile, start, rows, amount):
        at = (tile, pl.ds(start, rows))
        window[at] = (window[at].astype(jnp.float32) - amount.astype(jnp.float32)).astype(jnp.bfloat16)

    def own_tile(place, unit):
        return (place * 2 + y) * 3 + unit

    def mate_tile(place, unit):
        return (place * 2 + 1 - y) * 3 + unit

    def local_tile(unit):
        subtract(own_tile(z, unit), 0, TILE, product(factor(own[z, unit]), 0))
        subtract(mate_tile(z, unit), 0, TILE, product(factor(mate[unit]), 0))

    def place_of(d, s):
        return lax.rem(z + jnp.where(d == 0, 8 - s, s), 8)

    def sum_copy(place, unit, rows):
        return pltpu.make_async_remote_copy(
            sums_out.at[place, unit, pl.ds(0, rows)], sums_in.at[place, unit, pl.ds(0, rows)],
            sum_send.at[place, unit], sum_recv.at[place, unit], device_id=mate_dev, device_id_type=MESH,
        )

    def column_tile(place, unit):
        factors = factor(own[place, unit])
        sums_out[place, unit] = product(factors, 1).astype(jnp.bfloat16)

        @pl.when(unit != 2)
        def _():
            sum_copy(place, unit, TILE).start()

        @pl.when(unit == 2)
        def _():
            sum_copy(place, unit, plain).start()

        subtract(own_tile(place, unit), 0, TILE, product(factors, 0))

    def finish(place, unit):
        @pl.when(unit != 2)
        def _():
            sum_copy(place, unit, TILE).wait_recv()
            subtract(mate_tile(place, unit), 0, TILE, sums_in[place, unit])

        @pl.when(unit == 2)
        def _():
            sum_copy(place, unit, plain).wait_recv()
            subtract(mate_tile(place, unit), 0, plain, sums_in[place, unit, 0:plain])

    def shared_tile(place):
        subtract(mate_tile(place, 2), plain, SHARED, product(factor(shared[place]), 0))

    def pair(i, compute):
        s, unit = i // 3 + 1, lax.rem(i, 3)

        def one(d, carry):
            compute(place_of(d, s), unit)
            return carry

        lax.fori_loop(0, 2, one, 0)

    def visit(i, carry):
        s, unit = i // 3 + 1, lax.rem(i, 3)

        @pl.when(s > 1)
        def _():
            for d in (0, 1):
                arrived(d, s, unit)

                @pl.when(s == 2)
                def _():
                    ring_copy(d, s, unit).start()

                @pl.when(s == 3)
                def _():
                    opposite(next_place[d], lambda up: ring_copy(d, s, unit, up).start())

        pair(i, column_tile)

        @pl.when(i == 2)
        def _():
            column_tile(z, 2)

        @pl.when(i == 3)
        def _():
            mate_copy(0).wait_recv()
            mate_copy(1).wait_recv()

        @pl.when(jnp.logical_and(s == 2, unit != 2))
        def _():
            local_tile(unit)

        @pl.when(i == 5)
        def _():
            finish(z, 2)
            shared_tile(z)

        @pl.when(i > 2)
        def _():
            pair(i - 3, finish)

        @pl.when(unit == 2)
        def _():
            for d in (0, 1):
                arrived(d, s, 3)

                @pl.when(s < 3)
                def _():
                    ring_copy(d, s, 3).start()

                @pl.when(s == 3)
                def _():
                    opposite(next_place[d], lambda up: ring_copy(d, s, 3, up).start())

            def one(d, carry):
                shared_tile(place_of(d, s))
                return carry

            lax.fori_loop(0, 2, one, 0)

        return carry

    lax.fori_loop(0, 9, visit, 0)

    far = lax.rem(z + 4, 8)

    def last(unit, carry):
        for d in (0, 1):
            opposite(z, lambda up: arrived(d, 4, unit, up))
        column_tile(far, unit)

        pair(6 + unit, finish)
        return carry

    lax.fori_loop(0, 3, last, 0)
    for d in (0, 1):
        opposite(z, lambda up: arrived(d, 4, 3, up))
    shared_tile(far)
    for unit in range(3):
        finish(far, unit)

    for unit in range(4):
        if unit != 2:
            mate_copy(unit).wait_send()
        for d in (0, 1):
            for s in range(3):
                ring_copy(d, s, unit).wait_send()
            opposite(next_place[d], lambda up: ring_copy(d, 3, unit, up).wait_send())

    def drain(i, carry):
        place = lax.rem(z + i, 8)
        for unit in range(3):
            sum_copy(place, unit, plain if unit == 2 else TILE).wait_send()
        return carry

    lax.fori_loop(1, 8, drain, 0)
    sum_copy(z, 2, plain).wait_send()
    pltpu.make_async_copy(peers, peers, spread_sem.at[0]).wait()
    swap.wait_send()

    @pl.when(z == 0)
    def _():
        ref = pieces.at[pl.ds(0, 7)]
        pltpu.make_async_copy(ref, ref, piece_sem.at[4]).wait()

    @pl.when(is_source)
    def _():
        ref = own.at[0, 0, pl.ds(0, 240)]
        pltpu.make_async_copy(ref, ref, piece_sem.at[0]).wait()

    @pl.when(is_couple)
    def _():
        ref = pieces.at[pl.ds(0, 2 * PIECE - 1), :, pl.ds(512, 128)]
        pltpu.make_async_copy(ref, ref, piece_sem.at[2]).wait()


def shards(panel_cols, inverses, trailing):
    bf16 = jnp.bfloat16
    return pl.pallas_call(
        kernel,
        out_shape=pltpu.VMEM(trailing.shape, bf16),
        in_specs=[
            pl.BlockSpec(memory_space=pl.ANY),
            pl.BlockSpec(memory_space=pltpu.VMEM),
            pl.BlockSpec(memory_space=pl.ANY),
        ],
        out_specs=pl.BlockSpec(memory_space=pltpu.VMEM),
        scratch_shapes=[
            pltpu.VMEM((8, 3, TILE, 2 * TILE), bf16),
            pltpu.VMEM((2, TILE, 2 * TILE), bf16),
            pltpu.VMEM((8, SHARED, 2 * TILE), bf16),
            pltpu.VMEM((8, 3, TILE, TILE), bf16),
            pltpu.VMEM((8, 3, TILE, TILE), bf16),
            pltpu.VMEM((8, 16, 640), bf16),
            pltpu.VMEM((16, 128), bf16),
            pltpu.VMEM((2 * PIECE, 16, 640), bf16),
            pltpu.VMEM((TILE, TILE), bf16),
            pltpu.VMEM((2, TILE, 2 * TILE), bf16),
            pltpu.SemaphoreType.DMA((2, 4, 4)),
            pltpu.SemaphoreType.DMA((2, 4, 4)),
            pltpu.SemaphoreType.DMA((4,)),
            pltpu.SemaphoreType.DMA((4,)),
            pltpu.SemaphoreType.DMA((8, 3)),
            pltpu.SemaphoreType.DMA((8, 3)),
            pltpu.SemaphoreType.DMA((2,)),
            pltpu.SemaphoreType.DMA((6,)),
            pltpu.SemaphoreType.DMA((4,)),
            pltpu.SemaphoreType.REGULAR((4,)),
        ],
        compiler_params=pltpu.CompilerParams(
            collective_id=0, has_side_effects=True, vmem_limit_bytes=56 << 20
        ),
        name="panel_update",
    )(panel_cols, inverses, trailing)


def solution(mesh):
    in_specs = (P("col", "row", None), P(), P(None, "row", "col"))
    out_specs = P(None, "row", "col")
    return jax.shard_map(shards, mesh=mesh, in_specs=in_specs, out_specs=out_specs, check_vma=False)
```

profile of v0, /device:TPU:8, one launch (start us, length us, event | category | flops | bytes accessed | tf_op | source)
XLA Modules:
  0.0 87.5 jit_solution(3518224878509812366)
XLA Ops:
  0.0 84.8 %panel_update.1 = bf16[48,256,256]{2,1,0:T(8,128)(2,1)S(1)} custom-call(bf16[3,256,512]{2,1,0:T(8,128)(2,1)} %panel.1, bf16[2,256,256]{2,1,0:T(8,128)(2,1)} %inverses.1, bf16[48,256,256]{2,1,0:T(8,128)(2,1)} %trailing.1), custom_call_target="tpu_custom_call" | custom-call | tf_op jit(solution)/shard_map/panel_update/pallas_call | solution.py:512
  84.8 2.7 %copy.5 = bf16[48,256,256]{2,1,0:T(8,128)(2,1)} copy(bf16[48,256,256]{2,1,0:T(8,128)(2,1)S(1)} %panel_update.1) | data formatting | bytes 12582912
where the time goes:
time: 87.8 us; the launch traced here: 87.5 us
  Pallas kernels  84.8 us (97%)
  local copies, waits for them, and re-layouts  2.71 us (3%)
    pallas_call x1, Pallas kernels, shards(): pl.pallas_call(kernel, out_shape=pltpu.VMEM(trailing.shape, bf16), in_spe...  84.8 us
    unnamed x1, local copies, waits for them, and re-layouts  2.71 us

commit v1 on v0

--- a/solution.py
+++ b/solution.py
@@ -10,8 +10,8 @@
 MESH = pl.DeviceIdType.MESH
 TILE = 256
 SHARED = 112
-FIRST = 128
-FEWER = 112
+FIRST = 192
+FEWER = 128
 BEFORE = (3, 0)
 PIECE = 16
 
@@ -248,6 +248,7 @@
         for plane in range(8):
             stage[plane, :, 512:640] = couple_piece[...]
         pieces[my_piece] = stage[0]
+        spread()
         pl.semaphore_wait(ready_sem.at[1], 5)
 
         def send(plane, carry):
@@ -260,7 +261,6 @@
         lax.fori_loop(1, 8, send, 0)
         begin_part(FIRST, TILE - FIRST)
         begin((1, 2))
-        spread()
 
     def begin_beside(inward, outward):
         begin((0,), (inward,))

time: 87.8 us -> 87.6 us (level)
  no operation moved by 1% of the time
where the time goes in v1:
time: 87.6 us; the launch traced here: 87.5 us
  Pallas kernels  84.8 us (97%)
  local copies, waits for them, and re-layouts  2.71 us (3%)
    pallas_call x1, Pallas kernels, shards(): pl.pallas_call(kernel, out_shape=pltpu.VMEM(trailing.shape, bf16), in_spe...  84.8 us
    unnamed x1, local copies, waits for them, and re-layouts  2.71 us

profile of v1, /device:TPU:8, one launch (start us, length us, event | category | flops | bytes accessed | tf_op | source)
XLA Modules:
  0.0 87.5 jit_solution(1256796403070486307)
XLA Ops:
  0.0 84.8 %panel_update.1 = bf16[48,256,256]{2,1,0:T(8,128)(2,1)S(1)} custom-call(bf16[3,256,512]{2,1,0:T(8,128)(2,1)} %panel.1, bf16[2,256,256]{2,1,0:T(8,128)(2,1)} %inverses.1, bf16[48,256,256]{2,1,0:T(8,128)(2,1)} %trailing.1), custom_call_target="tpu_custom_call" | custom-call | tf_op jit(solution)/shard_map/panel_update/pallas_call | solution.py:512
  84.8 2.7 %copy.5 = bf16[48,256,256]{2,1,0:T(8,128)(2,1)} copy(bf16[48,256,256]{2,1,0:T(8,128)(2,1)S(1)} %panel_update.1) | data formatting | bytes 12582912
